TPU v7x, 32 devices: a whole 2x2x4 slice. The times are simulated.
32 devices in a mesh: grp: 2 (over x), samp: 16 (over z, y, core).
Axes of the slice: x: 2, y: 2, z: 4, core: 2. Of those that a mesh axis runs over, the one named last changes fastest.
Arguments:
- genotypes: int32 [32768, 2048], P(('grp', 'samp')), parts along dimension 0, may hold values from 0 to 2
- probe_signs: int32 [32, 32768], P(None, ('grp', 'samp')), parts along dimension 1, may hold values from 0 to 1
- phenotype: float32 [32768], P(('grp', 'samp')), parts along dimension 0, may hold values from -6 to 6
- marker_mean: float32 [2048], replicated, may hold values from 0.2 to 1.8
- marker_scale: float32 [2048], replicated, may hold values from 0.5 to 4
- marker_bin: int32 [2048], replicated, may hold values from 0 to 15, as said below
Outputs:
- products: float32 [16, 33, 32768], P(None, None, ('grp', 'samp')), parts along dimension 2
- gram: float32 [32, 16, 33], P('grp'), parts along dimension 0
There are 2 independent parts, one for each index of `grp`. A program takes and returns all parts, laid end to end along the dimension named above; an argument that names none is the same for every part. Nothing has to cross between parts.
Inputs may be any that keep to these rules, and one draw needn't show every extreme that they name: `marker_bin`: every bin holds exactly 128 markers.
All inputs are finite; a program needn't handle non-finite values.
Results may differ from a plain program's by a relative error of at most 0.0001.
Values sent between devices are 32-bit elements; how exact they have to be, the bound alone decides.
A program may use at most 128 MiB of HBM per device.

v0:
```python
import jax
import jax.numpy as jnp
from jax import lax
from jax.sharding import PartitionSpec as P

BINS = 16
M_BIN = 128


def shards(genotypes, probe_signs, phenotype, marker_mean, marker_scale, marker_bin):
    samples = genotypes.shape[0]
    devices = lax.axis_size("samp")
    total = jnp.float32(samples * devices)
    order = jnp.argsort(marker_bin, stable=True)
    picked = jnp.take(genotypes, order, axis=1).astype(jnp.float32)
    standard = (picked - marker_mean[order]) * marker_scale[order]
    vectors = jnp.concatenate(
        [(2 * probe_signs - 1).astype(jnp.float32), phenotype[None, :]], axis=0
    )
    share = lax.psum_scatter(
        jnp.dot(
            standard.T,
            vectors.T,
            precision=lax.Precision.HIGHEST,
            preferred_element_type=jnp.float32,
        ),
        "samp",
        scatter_dimension=0,
        tiled=True,
    )
    scores = lax.all_gather(share, "samp", axis=0, tiled=True)
    scores = scores / jnp.sqrt(total)
    blocks = standard.reshape(samples, BINS, M_BIN)
    weights = scores.reshape(BINS, M_BIN, scores.shape[1])
    products = jnp.einsum(
        "skm,kmr->krs", blocks, weights, precision=lax.Precision.HIGHEST
    ) / jnp.sqrt(jnp.float32(M_BIN))
    local_gram = jnp.einsum("krs,lrs->klr", products, products, precision=lax.Precision.HIGHEST)
    gram = lax.psum(local_gram, "samp") / total
    return (products, gram)


def solution(mesh):
    in_specs = (
        P(("grp", "samp"), None),
        P(None, ("grp", "samp")),
        P(("grp", "samp")),
        P(),
        P(),
        P(),
    )
    out_specs = (P(None, None, ("grp", "samp")), P("grp", None, None))
    return jax.shard_map(shards, mesh=mesh, in_specs=in_specs, out_specs=out_specs, check_vma=False)
```

profile of v0, /device:TPU:0, one launch (start us, length us, event | category | flops | bytes accessed | tf_op | source)
XLA Modules:
  0.0 233.8 jit_solution(9177498620670587703)
XLA Ops:
  7.2 0.0 copy-start
  7.2 0.0 copy-start.1
  7.2 0.0 reduce-scatter.2.cloned.1.call-start
  7.2 5.7 %sort.17 = (s32[2048]{0:T(1024)}, s32[2048]{0:T(1024)S(1)}) sort(s32[2048]{0:T(1024)} %param.11, s32[2048]{0:T(1024)S(1)} %iota.4), dimensions={0}, to_apply=%region_0.0 | sort | flops 22528 | bytes 32768 | tf_op jit(solution)/shard_map/jit(argsort)/sort | solution.py:14
  13.0 0.0 copy-done
  13.0 0.0 copy-start.3
  13.0 11.8 %gather_fusion.2 = f32[2048]{0:T(1024)S(1)} fusion(f32[2048]{0:T(1024)S(1)} %copy-done, s32[2048]{0:T(1024)S(1)} %fusion.25), kind=kCustom, calls=%fused_computation.2 | custom fusion | bytes 24576 | tf_op jit(solution)/shard_map/gather | solution.py:16
  24.8 0.0 copy-done.1
  24.8 11.8 %gather_fusion.1 = f32[2048]{0:T(1024)S(1)} fusion(f32[2048]{0:T(1024)S(1)} %copy-done.1, s32[2048]{0:T(1024)S(1)} %fusion.25), kind=kCustom, calls=%fused_computation.1 | custom fusion | bytes 24576 | tf_op jit(solution)/shard_map/gather | solution.py:16
  36.6 0.0 copy-done.3
  36.6 9.3 %copy.15 = s32[1024,2048]{0,1:T(8,128)} copy(s32[1024,2048]{1,0:T(8,128)} %param.6) | data formatting | bytes 16777216 | tf_op args[0]
  45.9 0.0 copy-start.4
  45.9 15.1 %gather_fusion = s32[2048,1024]{1,0:T(8,128)} fusion(s32[1024,2048]{0,1:T(8,128)} %copy.15, s32[2048]{0:T(1024)S(1)} %fusion.25), kind=kCustom, calls=%fused_computation | custom fusion | bytes 16785408 | tf_op jit(solution)/shard_map/jit(_take)/gather | solution.py:15
  61.1 0.0 copy-done.4
  61.1 12.3 %fusion.3 = f32[2048,33]{0,1:T(8,128)} fusion(s32[2048,1024]{1,0:T(8,128)} %gather_fusion, f32[2048]{0:T(1024)S(1)} %gather_fusion.2, f32[2048]{0:T(1024)S(1)} %gather_fusion.1, pred[2048]{0:T(1024)(128)(4,1)S(1)} %compare_and_fusion, f32[1,1024]{1,0:T(1,128)S(1)} %bitcast.31, f32[32,1024]{1,0:T(8,128)S(1)} %add_convert_fusion), kind=kOutput, calls=%fused_computation.7 | convolution fusion | flops 838894592 | bytes 8812544 | tf_op jit(solution)/shard_map/dot_general | solution.py:21
  73.3 0.0 reduce-scatter.2.cloned.1.call-update
  73.4 9.3 %copy.16 = s32[1024,16,128]{2,0,1:T(8,128)} copy(s32[1024,16,128]{0,2,1:T(8,128)} %bitcast.26) | data formatting | bytes 16777216 | tf_op jit(solution)/shard_map/jit(_take)/gather | solution.py:15
  82.6 45.9 %reduce-scatter.2.cloned.1.call-done = f32[128,33]{0,1:T(8,128)} async-done(((f32[2048,33]{0,1:T(8,128)}), f32[128,33]{0,1:T(8,128)}) %reduce-scatter.2.cloned.1.call-update) | async-done | bytes 16912 | tf_op jit(solution)/shard_map/reduce_scatter | solution.py:20
  128.6 20.7 %all_gather.3 = f32[2048,33]{0,1:T(8,128)S(1)} all-gather(f32[128,33]{0,1:T(8,128)} %reduce-scatter.2.cloned.1.call-done), channel_id=1, replica_groups=mesh['grp'=2,'samp'=16] {'samp'}, dimensions={0}, use_global_device_ids=true | all-gather | bytes 287232 | tf_op jit(solution)/shard_map/all_gather | solution.py:31
  149.3 0.1 copy.22
  149.4 11.3 %fusion.18 = f32[16,33,1024]{2,1,0:T(8,128)S(1)} fusion(s32[1024,16,128]{2,0,1:T(8,128)} %copy.16, f32[16,128]{1,0:T(8,128)S(1)} %bitcast.29, f32[16,128]{1,0:T(8,128)S(1)} %bitcast.30, pred[16,128]{1,0:T(8,128)(4,1)S(1)} %fusion.31, f32[16,128,33]{1,0,2:T(8,128)S(1)} %slice_bitcast_fusion), kind=kOutput, calls=%fused_computation.21 | convolution fusion | flops 839401472 | bytes 10840064 | tf_op jit(solution)/shard_map/skm,kmr->krs/dot_general | solution.py:35
  160.7 1.3 copy.20
  161.9 0.0 copy-start.2
  162.0 3.1 %convolution_bitcast_fusion = f32[16,16,33]{0,1,2:T(8,128)S(1)} fusion(f32[16,33,1024]{2,0,1:T(8,128)S(1)} %copy.20), kind=kOutput, calls=%fused_computation.22 | convolution fusion | flops 103809024 | bytes 2196480 | tf_op jit(solution)/shard_map/krs,lrs->klr/dot_general | solution.py:38
  165.1 61.0 %psum.7 = f32[16,16,33]{0,1,2:T(8,128)S(1)} all-reduce(f32[16,16,33]{0,1,2:T(8,128)S(1)} %convolution_bitcast_fusion), channel_id=1, replica_groups=mesh['grp'=2,'samp'=16] {'samp'}, use_global_device_ids=true, to_apply=%region_2.3 | all-reduce | flops 8448 | bytes 67584 | tf_op jit(solution)/shard_map/psum | solution.py:39
  226.1 0.8 copy.21
  227.0 0.0 copy-done.2
  (8 shorter events, 0.1 us)
Async XLA Ops:
  7.2 5.8 %copy-start = (f32[2048]{0:T(1024)S(1)}, f32[2048]{0:T(1024)}, u32[]{:S(2)}) copy-start(f32[2048]{0:T(1024)} %param.10) | copy-start | bytes 24580
  7.2 17.6 %copy-start.1 = (f32[2048]{0:T(1024)S(1)}, f32[2048]{0:T(1024)}, u32[]{:S(2)}) copy-start(f32[2048]{0:T(1024)} %param.9) | copy-start | bytes 24580
  7.2 121.4 %reduce-scatter.2.cloned.1.call-start = ((), (), s32[]{:S(2)}) async-start(), calls=%async_computation.1 | async-start | bytes 348160 | tf_op jit(solution)/shard_map/reduce_scatter | solution.py:20
  13.0 23.6 %copy-start.3 = (s32[32,1024]{1,0:T(8,128)S(1)}, s32[32,1024]{1,0:T(8,128)}, u32[]{:S(2)}) copy-start(s32[32,1024]{1,0:T(8,128)} %param.7) | copy-start | bytes 393220
  45.9 15.2 %copy-start.4 = (f32[1024]{0:T(1024)S(1)}, f32[1024]{0:T(1024)}, u32[]{:S(2)}) copy-start(f32[1024]{0:T(1024)} %param.8) | copy-start | bytes 12292
  161.9 65.0 %copy-start.2 = (f32[16,33,1024]{2,0,1:T(8,128)}, f32[16,33,1024]{2,0,1:T(8,128)S(1)}, u32[]{:S(2)}) copy-start(f32[16,33,1024]{2,0,1:T(8,128)S(1)} %copy.20) | copy-start | bytes 6488068
Sparse Core Ops, SparseCore 0:
  73.5 55.0 reduce-scatter.1
where the time goes:
time: 234 us
  blocking collectives  81.7 us (35%)
  local copies, waits for them, and re-layouts  59.5 us (25%)
  waiting for transfers between devices  45.9 us (20%)
  matrix products  26.7 us (11%)
  between operations  14.2 us (6%)
  other arithmetic  5.82 us (2%)
    psum x1, blocking collectives, shards(): gram = lax.psum(local_gram, 'samp') / total  61 us
    reduce_scatter x1, waiting for transfers between devices, shards(): lax.psum_scatter(jnp.dot(standard.T, vectors.T, precision=lax.Precision.H...  45.9 us
    gather x2, local copies, waits for them, and re-layouts, shards(): picked = jnp.take(genotypes, order, axis=1).astype(jnp.float32)  24.4 us
    gather x2, local copies, waits for them, and re-layouts, shards(): standard = (picked - marker_mean[order]) * marker_scale[order]  23.6 us
    all_gather x1, blocking collectives, shards(): scores = lax.all_gather(share, 'samp', axis=0, tiled=True)  20.7 us
    dot_general x1, matrix products, shards(): jnp.dot(standard.T, vectors.T, precision=lax.Precision.HIGHEST, preferred...  12.3 us
    unnamed x14, local copies, waits for them, and re-layouts  11.5 us
    dot_general x1, matrix products, shards(): jnp.einsum('skm,kmr->krs', blocks, weights, precision=lax.Precision.HIGHEST)  11.3 us
  transfers between devices with their start and end apart: 1, of which 1 were waited for; matrix products, arithmetic and copies ran while one was open for 4% of the time, Pallas kernels for 0%

commit v1 on v0

--- a/solution.py
+++ b/solution.py
@@ -5,6 +5,19 @@
 
 BINS = 16
 M_BIN = 128
+
+
+def collect(array, axis, dim):
+    devices, index, extent = (lax.axis_size(axis), lax.axis_index(axis), array.shape[dim])
+    forward = [(i, (i + 1) % devices) for i in range(devices)]
+    whole = jnp.zeros((*array.shape[:dim], devices * extent, *array.shape[dim + 1 :]), array.dtype)
+    held = array
+    for step in range(devices):
+        owner = (index - step) % devices
+        whole = lax.dynamic_update_slice_in_dim(whole, held, owner * extent, axis=dim)
+        if step < devices - 1:
+            held = lax.ppermute(held, axis, forward)
+    return whole
 
 
 def shards(genotypes, probe_signs, phenotype, marker_mean, marker_scale, marker_bin):
@@ -28,7 +41,7 @@
         scatter_dimension=0,
         tiled=True,
     )
-    scores = lax.all_gather(share, "samp", axis=0, tiled=True)
+    scores = collect(share, "samp", 0)
     scores = scores / jnp.sqrt(total)
     blocks = standard.reshape(samples, BINS, M_BIN)
     weights = scores.reshape(BINS, M_BIN, scores.shape[1])

time: 234 us -> 302 us (1.29)
  waiting for transfers between devices: 45.9 us -> 134 us
  blocking collectives: 81.7 us -> 60.7 us
    ppermute x0 -> x15, waiting for transfers between devices: none -> 87.9 us  [collect(): held = lax.ppermute(held, axis, forward)]
    all_gather x1 -> x0, blocking collectives: 20.7 us -> none  [shards(): scores = lax.all_gather(share, 'samp', axis=0, tiled=True)]
  transfers between devices with their start and end apart: 1 -> 16, of which waited for: 1 -> 16; matrix products, arithmetic and copies ran while one was open for 4% -> 3% of each run, Pallas kernels for 0% -> 0%
where the time goes in v1:
time: 302 us
  waiting for transfers between devices  134 us (44%)
  blocking collectives  60.7 us (20%)
  local copies, waits for them, and re-layouts  60.2 us (20%)
  matrix products  26.7 us (9%)
  between operations  14.5 us (5%)
  other arithmetic  5.82 us (2%)
    ppermute x15, waiting for transfers between devices, collect(): held = lax.ppermute(held, axis, forward)  87.9 us
    psum x1, blocking collectives, shards(): gram = lax.psum(local_gram, 'samp') / total  60.7 us
    reduce_scatter x1, waiting for transfers between devices, shards(): lax.psum_scatter(jnp.dot(standard.T, vectors.T, precision=lax.Precision.H...  45.7 us
    gather x2, local copies, waits for them, and re-layouts, shards(): picked = jnp.take(genotypes, order, axis=1).astype(jnp.float32)  24.4 us
    gather x2, local copies, waits for them, and re-layouts, shards(): standard = (picked - marker_mean[order]) * marker_scale[order]  23.6 us
    dot_general x1, matrix products, shards(): jnp.dot(standard.T, vectors.T, precision=lax.Precision.HIGHEST, preferred...  12.3 us
    unnamed x14, local copies, waits for them, and re-layouts  11.4 us
    dot_general x1, matrix products, shards(): jnp.einsum('skm,kmr->krs', blocks, weights, precision=lax.Precision.HIGHEST)  11.3 us
  transfers between devices with their start and end apart: 16, of which 16 were waited for; matrix products, arithmetic and copies ran while one was open for 3% of the time, Pallas kernels for 0%

profile of v1, /device:TPU:0, one launch (start us, length us, event | category | flops | bytes accessed | tf_op | source)
XLA Modules:
  0.0 301.5 jit_solution(10872221180139865947)
XLA Ops:
  7.2 0.0 copy-start
  7.2 0.0 reduce-scatter.2.cloned.1.call-start
  7.2 5.7 %sort.17 = (s32[2048]{0:T(1024)}, s32[2048]{0:T(1024)S(1)}) sort(s32[2048]{0:T(1024)} %param.11, s32[2048]{0:T(1024)S(1)} %iota.4), dimensions={0}, to_apply=%region_0.0 | sort | flops 22528 | bytes 32768 | tf_op jit(solution)/shard_map/jit(argsort)/sort | solution.py:27
  13.0 9.2 %copy.14 = s32[1024,2048]{0,1:T(8,128)} copy(s32[1024,2048]{1,0:T(8,128)} %param.6) | data formatting | bytes 16777216 | tf_op args[0]
  22.2 15.1 %gather_fusion = s32[2048,1024]{1,0:T(8,128)} fusion(s32[1024,2048]{0,1:T(8,128)} %copy.14, s32[2048]{0:T(1024)S(1)} %fusion.25), kind=kCustom, calls=%fused_computation | custom fusion | bytes 16785408 | tf_op jit(solution)/shard_map/jit(_take)/gather | solution.py:28
  37.4 0.0 copy-start.4
  37.4 11.8 %gather_fusion.1 = f32[2048]{0:T(1024)S(1)} fusion(f32[2048]{0:T(1024)S(1)} %copy-done, s32[2048]{0:T(1024)S(1)} %fusion.25), kind=kCustom, calls=%fused_computation.1 | custom fusion | bytes 24576 | tf_op jit(solution)/shard_map/gather | solution.py:29
  49.2 11.8 %gather_fusion.2 = f32[2048]{0:T(1024)S(1)} fusion(f32[2048]{0:T(1024)S(1)} %copy-done.1, s32[2048]{0:T(1024)S(1)} %fusion.25), kind=kCustom, calls=%fused_computation.2 | custom fusion | bytes 24576 | tf_op jit(solution)/shard_map/gather | solution.py:29
  61.0 12.3 %fusion.3 = f32[2048,33]{0,1:T(8,128)} fusion(s32[2048,1024]{1,0:T(8,128)} %gather_fusion, f32[2048]{0:T(1024)S(1)} %gather_fusion.2, f32[2048]{0:T(1024)S(1)} %gather_fusion.1, pred[2048]{0:T(1024)(128)(4,1)S(1)} %compare_and_fusion, f32[1,1024]{1,0:T(1,128)S(1)} %bitcast.31, f32[32,1024]{1,0:T(8,128)S(1)} %add_convert_fusion), kind=kOutput, calls=%fused_computation.7 | convolution fusion | flops 838894592 | bytes 8812544 | tf_op jit(solution)/shard_map/dot_general | solution.py:34
  73.3 0.0 reduce-scatter.2.cloned.1.call-update
  73.6 9.2 %copy.15 = s32[1024,16,128]{2,0,1:T(8,128)} copy(s32[1024,16,128]{0,2,1:T(8,128)} %bitcast.26) | data formatting | bytes 16777216 | tf_op jit(solution)/shard_map/jit(_take)/gather | solution.py:28
  82.9 45.7 %reduce-scatter.2.cloned.1.call-done = f32[128,33]{0,1:T(8,128)} async-done(((f32[2048,33]{0,1:T(8,128)}), f32[128,33]{0,1:T(8,128)}) %reduce-scatter.2.cloned.1.call-update) | async-done | bytes 16912 | tf_op jit(solution)/shard_map/reduce_scatter | solution.py:33
  128.5 0.0 collective-permute-start
  128.6 0.7 constant_dynamic-update-slice_fusion.15
  129.3 5.3 %collective-permute-done = f32[128,33]{0,1:T(8,128)S(1)} collective-permute-done((f32[128,33]{0,1:T(8,128)}, f32[128,33]{0,1:T(8,128)S(1)}, u32[]{:S(2)}, u32[]{:S(2)}) %collective-permute-start) | collective-permute-done | bytes 16928 | tf_op jit(solution)/shard_map/ppermute | solution.py:19
  134.6 0.0 collective-permute-start.1
  134.7 5.9 %collective-permute-done.1 = f32[128,33]{0,1:T(8,128)S(1)} collective-permute-done((f32[128,33]{0,1:T(8,128)S(1)}, f32[128,33]{0,1:T(8,128)S(1)}, u32[]{:S(2)}, u32[]{:S(2)}) %collective-permute-start.1) | collective-permute-done | bytes 16928 | tf_op jit(solution)/shard_map/ppermute | solution.py:19
  140.6 0.0 collective-permute-start.2
  140.6 5.9 %collective-permute-done.2 = f32[128,33]{0,1:T(8,128)S(1)} collective-permute-done((f32[128,33]{0,1:T(8,128)S(1)}, f32[128,33]{0,1:T(8,128)S(1)}, u32[]{:S(2)}, u32[]{:S(2)}) %collective-permute-start.2) | collective-permute-done | bytes 16928 | tf_op jit(solution)/shard_map/ppermute | solution.py:19
  146.5 0.0 collective-permute-start.3
  146.5 5.9 %collective-permute-done.3 = f32[128,33]{0,1:T(8,128)S(1)} collective-permute-done((f32[128,33]{0,1:T(8,128)S(1)}, f32[128,33]{0,1:T(8,128)S(1)}, u32[]{:S(2)}, u32[]{:S(2)}) %collective-permute-start.3) | collective-permute-done | bytes 16928 | tf_op jit(solution)/shard_map/ppermute | solution.py:19
  152.4 0.0 collective-permute-start.4
  152.4 5.9 %collective-permute-done.4 = f32[128,33]{0,1:T(8,128)S(1)} collective-permute-done((f32[128,33]{0,1:T(8,128)S(1)}, f32[128,33]{0,1:T(8,128)S(1)}, u32[]{:S(2)}, u32[]{:S(2)}) %collective-permute-start.4) | collective-permute-done | bytes 16928 | tf_op jit(solution)/shard_map/ppermute | solution.py:19
  158.3 0.0 collective-permute-start.5
  158.3 5.9 %collective-permute-done.5 = f32[128,33]{0,1:T(8,128)S(1)} collective-permute-done((f32[128,33]{0,1:T(8,128)S(1)}, f32[128,33]{0,1:T(8,128)S(1)}, u32[]{:S(2)}, u32[]{:S(2)}) %collective-permute-start.5) | collective-permute-done | bytes 16928 | tf_op jit(solution)/shard_map/ppermute | solution.py:19
  164.2 0.0 collective-permute-start.6
  164.2 5.9 %collective-permute-done.6 = f32[128,33]{0,1:T(8,128)S(1)} collective-permute-done((f32[128,33]{0,1:T(8,128)S(1)}, f32[128,33]{0,1:T(8,128)S(1)}, u32[]{:S(2)}, u32[]{:S(2)}) %collective-permute-start.6) | collective-permute-done | bytes 16928 | tf_op jit(solution)/shard_map/ppermute | solution.py:19
  170.1 0.0 collective-permute-start.7
  170.1 5.9 %collective-permute-done.7 = f32[128,33]{0,1:T(8,128)S(1)} collective-permute-done((f32[128,33]{0,1:T(8,128)S(1)}, f32[128,33]{0,1:T(8,128)S(1)}, u32[]{:S(2)}, u32[]{:S(2)}) %collective-permute-start.7) | collective-permute-done | bytes 16928 | tf_op jit(solution)/shard_map/ppermute | solution.py:19
  176.0 5.9 %collective-permute-done.8 = f32[128,33]{0,1:T(8,128)S(1)} collective-permute-done((f32[128,33]{0,1:T(8,128)S(1)}, f32[128,33]{0,1:T(8,128)S(1)}, u32[]{:S(2)}, u32[]{:S(2)}) %collective-permute-start.8) | collective-permute-done | bytes 16928 | tf_op jit(solution)/shard_map/ppermute | solution.py:19
  181.9 5.9 %collective-permute-done.9 = f32[128,33]{0,1:T(8,128)S(1)} collective-permute-done((f32[128,33]{0,1:T(8,128)S(1)}, f32[128,33]{0,1:T(8,128)S(1)}, u32[]{:S(2)}, u32[]{:S(2)}) %collective-permute-start.9) | collective-permute-done | bytes 16928 | tf_op jit(solution)/shard_map/ppermute | solution.py:19
  187.8 0.0 collective-permute-start.10
  187.8 5.9 %collective-permute-done.10 = f32[128,33]{0,1:T(8,128)S(1)} collective-permute-done((f32[128,33]{0,1:T(8,128)S(1)}, f32[128,33]{0,1:T(8,128)S(1)}, u32[]{:S(2)}, u32[]{:S(2)}) %collective-permute-start.10) | collective-permute-done | bytes 16928 | tf_op jit(solution)/shard_map/ppermute | solution.py:19
  193.7 0.0 collective-permute-start.11
  193.7 5.9 %collective-permute-done.11 = f32[128,33]{0,1:T(8,128)S(1)} collective-permute-done((f32[128,33]{0,1:T(8,128)S(1)}, f32[128,33]{0,1:T(8,128)S(1)}, u32[]{:S(2)}, u32[]{:S(2)}) %collective-permute-start.11) | collective-permute-done | bytes 16928 | tf_op jit(solution)/shard_map/ppermute | solution.py:19
  199.6 0.0 collective-permute-start.12
  199.6 5.9 %collective-permute-done.12 = f32[128,33]{0,1:T(8,128)S(1)} collective-permute-done((f32[128,33]{0,1:T(8,128)S(1)}, f32[128,33]{0,1:T(8,128)S(1)}, u32[]{:S(2)}, u32[]{:S(2)}) %collective-permute-start.12) | collective-permute-done | bytes 16928 | tf_op jit(solution)/shard_map/ppermute | solution.py:19
  205.5 0.0 collective-permute-start.13
  205.5 5.9 %collective-permute-done.13 = f32[128,33]{0,1:T(8,128)S(1)} collective-permute-done((f32[128,33]{0,1:T(8,128)S(1)}, f32[128,33]{0,1:T(8,128)S(1)}, u32[]{:S(2)}, u32[]{:S(2)}) %collective-permute-start.13) | collective-permute-done | bytes 16928 | tf_op jit(solution)/shard_map/ppermute | solution.py:19
  211.4 0.0 collective-permute-start.14
  211.4 5.9 %collective-permute-done.14 = f32[128,33]{0,1:T(8,128)S(1)} collective-permute-done((f32[128,33]{0,1:T(8,128)S(1)}, f32[128,33]{0,1:T(8,128)S(1)}, u32[]{:S(2)}, u32[]{:S(2)}) %collective-permute-start.14) | collective-permute-done | bytes 16928 | tf_op jit(solution)/shard_map/ppermute | solution.py:19
  217.4 0.1 copy.21
  217.5 11.3 %fusion.18 = f32[16,33,1024]{2,1,0:T(8,128)S(1)} fusion(s32[1024,16,128]{2,0,1:T(8,128)} %copy.15, f32[16,128]{1,0:T(8,128)S(1)} %bitcast.30, f32[16,128]{1,0:T(8,128)S(1)} %bitcast.29, pred[16,128]{1,0:T(8,128)(4,1)S(1)} %fusion.31, f32[16,128,33]{1,0,2:T(8,128)S(1)} %slice_bitcast_fusion), kind=kOutput, calls=%fused_computation.21 | convolution fusion | flops 839401472 | bytes 10840064 | tf_op jit(solution)/shard_map/skm,kmr->krs/dot_general | solution.py:48
  228.7 1.3 copy.19
  230.0 0.0 copy-start.2
  230.0 3.1 %convolution_bitcast_fusion = f32[16,16,33]{0,1,2:T(8,128)S(1)} fusion(f32[16,33,1024]{2,0,1:T(8,128)S(1)} %copy.19), kind=kOutput, calls=%fused_computation.22 | convolution fusion | flops 103809024 | bytes 2196480 | tf_op jit(solution)/shard_map/krs,lrs->klr/dot_general | solution.py:51
  233.1 60.7 %psum.7 = f32[16,16,33]{0,1,2:T(8,128)S(1)} all-reduce(f32[16,16,33]{0,1,2:T(8,128)S(1)} %convolution_bitcast_fusion), channel_id=1, replica_groups=mesh['grp'=2,'samp'=16] {'samp'}, use_global_device_ids=true, to_apply=%region_2.3 | all-reduce | flops 8448 | bytes 67584 | tf_op jit(solution)/shard_map/psum | solution.py:52
  293.8 0.8 copy.20
  (33 shorter events, 0.2 us)
Async XLA Ops:
  7.2 30.2 %copy-start = (f32[2048]{0:T(1024)S(1)}, f32[2048]{0:T(1024)}, u32[]{:S(2)}) copy-start(f32[2048]{0:T(1024)} %param.9) | copy-start | bytes 24580
  7.2 121.4 %reduce-scatter.2.cloned.1.call-start = ((), (), s32[]{:S(2)}) async-start(), calls=%async_computation.1 | async-start | bytes 348160 | tf_op jit(solution)/shard_map/reduce_scatter | solution.py:33
  37.4 11.8 %copy-start.1 = (f32[2048]{0:T(1024)S(1)}, f32[2048]{0:T(1024)}, u32[]{:S(2)}) copy-start(f32[2048]{0:T(1024)} %param.10) | copy-start | bytes 24580
  37.4 23.6 %copy-start.3 = (s32[32,1024]{1,0:T(8,128)S(1)}, s32[32,1024]{1,0:T(8,128)}, u32[]{:S(2)}) copy-start(s32[32,1024]{1,0:T(8,128)} %param.7) | copy-start | bytes 393220
  37.4 23.6 %copy-start.4 = (f32[1024]{0:T(1024)S(1)}, f32[1024]{0:T(1024)}, u32[]{:S(2)}) copy-start(f32[1024]{0:T(1024)} %param.8) | copy-start | bytes 12292
  128.5 6.1 %collective-permute-start = (f32[128,33]{0,1:T(8,128)}, f32[128,33]{0,1:T(8,128)S(1)}, u32[]{:S(2)}, u32[]{:S(2)}) collective-permute-start(f32[128,33]{0,1:T(8,128)} %reduce-scatter.2.cloned.1.call-done), channel_id=1, source_target_pairs={{0,1},{1,2},{2,3},{3,4},{4,5},{5,6},{6,7},{7,8},{8,9},{9,10},{10,1... | collective-permute-start | bytes 50696 | tf_op jit(solution)/shard_map/ppermute | solution.py:19
  134.6 5.9 %collective-permute-start.1 = (f32[128,33]{0,1:T(8,128)S(1)}, f32[128,33]{0,1:T(8,128)S(1)}, u32[]{:S(2)}, u32[]{:S(2)}) collective-permute-start(f32[128,33]{0,1:T(8,128)S(1)} %collective-permute-done), channel_id=1, source_target_pairs={{0,1},{1,2},{2,3},{3,4},{4,5},{5,6},{6,7},{7,8},{8,9},{9,10},{10,1... | collective-permute-start | bytes 50696 | tf_op jit(solution)/shard_map/ppermute | solution.py:19
  140.6 5.9 %collective-permute-start.2 = (f32[128,33]{0,1:T(8,128)S(1)}, f32[128,33]{0,1:T(8,128)S(1)}, u32[]{:S(2)}, u32[]{:S(2)}) collective-permute-start(f32[128,33]{0,1:T(8,128)S(1)} %collective-permute-done.1), channel_id=1, source_target_pairs={{0,1},{1,2},{2,3},{3,4},{4,5},{5,6},{6,7},{7,8},{8,9},{9,10},{10,1... | collective-permute-start | bytes 50696 | tf_op jit(solution)/shard_map/ppermute | solution.py:19
  146.5 5.9 %collective-permute-start.3 = (f32[128,33]{0,1:T(8,128)S(1)}, f32[128,33]{0,1:T(8,128)S(1)}, u32[]{:S(2)}, u32[]{:S(2)}) collective-permute-start(f32[128,33]{0,1:T(8,128)S(1)} %collective-permute-done.2), channel_id=1, source_target_pairs={{0,1},{1,2},{2,3},{3,4},{4,5},{5,6},{6,7},{7,8},{8,9},{9,10},{10,1... | collective-permute-start | bytes 50696 | tf_op jit(solution)/shard_map/ppermute | solution.py:19
  152.4 5.9 %collective-permute-start.4 = (f32[128,33]{0,1:T(8,128)S(1)}, f32[128,33]{0,1:T(8,128)S(1)}, u32[]{:S(2)}, u32[]{:S(2)}) collective-permute-start(f32[128,33]{0,1:T(8,128)S(1)} %collective-permute-done.3), channel_id=1, source_target_pairs={{0,1},{1,2},{2,3},{3,4},{4,5},{5,6},{6,7},{7,8},{8,9},{9,10},{10,1... | collective-permute-start | bytes 50696 | tf_op jit(solution)/shard_map/ppermute | solution.py:19
  158.3 5.9 %collective-permute-start.5 = (f32[128,33]{0,1:T(8,128)S(1)}, f32[128,33]{0,1:T(8,128)S(1)}, u32[]{:S(2)}, u32[]{:S(2)}) collective-permute-start(f32[128,33]{0,1:T(8,128)S(1)} %collective-permute-done.4), channel_id=1, source_target_pairs={{0,1},{1,2},{2,3},{3,4},{4,5},{5,6},{6,7},{7,8},{8,9},{9,10},{10,1... | collective-permute-start | bytes 50696 | tf_op jit(solution)/shard_map/ppermute | solution.py:19
  164.2 5.9 %collective-permute-start.6 = (f32[128,33]{0,1:T(8,128)S(1)}, f32[128,33]{0,1:T(8,128)S(1)}, u32[]{:S(2)}, u32[]{:S(2)}) collective-permute-start(f32[128,33]{0,1:T(8,128)S(1)} %collective-permute-done.5), channel_id=1, source_target_pairs={{0,1},{1,2},{2,3},{3,4},{4,5},{5,6},{6,7},{7,8},{8,9},{9,10},{10,1... | collective-permute-start | bytes 50696 | tf_op jit(solution)/shard_map/ppermute | solution.py:19
  170.1 5.9 %collective-permute-start.7 = (f32[128,33]{0,1:T(8,128)S(1)}, f32[128,33]{0,1:T(8,128)S(1)}, u32[]{:S(2)}, u32[]{:S(2)}) collective-permute-start(f32[128,33]{0,1:T(8,128)S(1)} %collective-permute-done.6), channel_id=1, source_target_pairs={{0,1},{1,2},{2,3},{3,4},{4,5},{5,6},{6,7},{7,8},{8,9},{9,10},{10,1... | collective-permute-start | bytes 50696 | tf_op jit(solution)/shard_map/ppermute | solution.py:19
  176.0 5.9 %collective-permute-start.8 = (f32[128,33]{0,1:T(8,128)S(1)}, f32[128,33]{0,1:T(8,128)S(1)}, u32[]{:S(2)}, u32[]{:S(2)}) collective-permute-start(f32[128,33]{0,1:T(8,128)S(1)} %collective-permute-done.7), channel_id=1, source_target_pairs={{0,1},{1,2},{2,3},{3,4},{4,5},{5,6},{6,7},{7,8},{8,9},{9,10},{10,1... | collective-permute-start | bytes 50696 | tf_op jit(solution)/shard_map/ppermute | solution.py:19
  181.9 5.9 %collective-permute-start.9 = (f32[128,33]{0,1:T(8,128)S(1)}, f32[128,33]{0,1:T(8,128)S(1)}, u32[]{:S(2)}, u32[]{:S(2)}) collective-permute-start(f32[128,33]{0,1:T(8,128)S(1)} %collective-permute-done.8), channel_id=1, source_target_pairs={{0,1},{1,2},{2,3},{3,4},{4,5},{5,6},{6,7},{7,8},{8,9},{9,10},{10,1... | collective-permute-start | bytes 50696 | tf_op jit(solution)/shard_map/ppermute | solution.py:19
  187.8 5.9 %collective-permute-start.10 = (f32[128,33]{0,1:T(8,128)S(1)}, f32[128,33]{0,1:T(8,128)S(1)}, u32[]{:S(2)}, u32[]{:S(2)}) collective-permute-start(f32[128,33]{0,1:T(8,128)S(1)} %collective-permute-done.9), channel_id=1, source_target_pairs={{0,1},{1,2},{2,3},{3,4},{4,5},{5,6},{6,7},{7,8},{8,9},{9,10},{10,1... | collective-permute-start | bytes 50696 | tf_op jit(solution)/shard_map/ppermute | solution.py:19
  193.7 5.9 %collective-permute-start.11 = (f32[128,33]{0,1:T(8,128)S(1)}, f32[128,33]{0,1:T(8,128)S(1)}, u32[]{:S(2)}, u32[]{:S(2)}) collective-permute-start(f32[128,33]{0,1:T(8,128)S(1)} %collective-permute-done.10), channel_id=1, source_target_pairs={{0,1},{1,2},{2,3},{3,4},{4,5},{5,6},{6,7},{7,8},{8,9},{9,10},{10,1... | collective-permute-start | bytes 50696 | tf_op jit(solution)/shard_map/ppermute | solution.py:19
  199.6 5.9 %collective-permute-start.12 = (f32[128,33]{0,1:T(8,128)S(1)}, f32[128,33]{0,1:T(8,128)S(1)}, u32[]{:S(2)}, u32[]{:S(2)}) collective-permute-start(f32[128,33]{0,1:T(8,128)S(1)} %collective-permute-done.11), channel_id=1, source_target_pairs={{0,1},{1,2},{2,3},{3,4},{4,5},{5,6},{6,7},{7,8},{8,9},{9,10},{10,1... | collective-permute-start | bytes 50696 | tf_op jit(solution)/shard_map/ppermute | solution.py:19
  205.5 5.9 %collective-permute-start.13 = (f32[128,33]{0,1:T(8,128)S(1)}, f32[128,33]{0,1:T(8,128)S(1)}, u32[]{:S(2)}, u32[]{:S(2)}) collective-permute-start(f32[128,33]{0,1:T(8,128)S(1)} %collective-permute-done.12), channel_id=1, source_target_pairs={{0,1},{1,2},{2,3},{3,4},{4,5},{5,6},{6,7},{7,8},{8,9},{9,10},{10,1... | collective-permute-start | bytes 50696 | tf_op jit(solution)/shard_map/ppermute | solution.py:19
  211.4 5.9 %collective-permute-start.14 = (f32[128,33]{0,1:T(8,128)S(1)}, f32[128,33]{0,1:T(8,128)S(1)}, u32[]{:S(2)}, u32[]{:S(2)}) collective-permute-start(f32[128,33]{0,1:T(8,128)S(1)} %collective-permute-done.13), channel_id=1, source_target_pairs={{0,1},{1,2},{2,3},{3,4},{4,5},{5,6},{6,7},{7,8},{8,9},{9,10},{10,1... | collective-permute-start | bytes 50696 | tf_op jit(solution)/shard_map/ppermute | solution.py:19
  230.0 64.7 %copy-start.2 = (f32[16,33,1024]{2,0,1:T(8,128)}, f32[16,33,1024]{2,0,1:T(8,128)S(1)}, u32[]{:S(2)}) copy-start(f32[16,33,1024]{2,0,1:T(8,128)S(1)} %copy.19) | copy-start | bytes 6488068
Sparse Core Ops, SparseCore 0:
  73.5 55.0 reduce-scatter.1
